TPU v7x, 32 devices: a whole 2x2x4 slice. The times are simulated.
32 devices in a mesh: groups: 2 (over y), dap: 4 (over z), chan: 2 (over x), sub: 2 (over core).
Axes of the slice: x: 2, y: 2, z: 4, core: 2. Of those that a mesh axis runs over, the one named last changes fastest.
Arguments:
- pair_input: bfloat16 [768, 384, 128], P(('groups', 'dap'), ('chan', 'sub')), parts along dimension 0, may hold values from -6 to 6
- first_gain: float32 [128], replicated, may hold values from 0.25 to 1.75
- first_project: bfloat16 [128, 512], replicated, may hold values from -0.5 to 0.5
- first_gate: bfloat16 [128, 128], replicated, may hold values from -0.5 to 0.5
- first_norm: float32 [128], replicated, may hold values from 0.25 to 1.75
- first_final: bfloat16 [128, 128], replicated, may hold values from -0.5 to 0.5
- second_gain: float32 [128], replicated, may hold values from 0.25 to 1.75
- second_project: bfloat16 [128, 512], replicated, may hold values from -0.5 to 0.5
- second_gate: bfloat16 [128, 128], replicated, may hold values from -0.5 to 0.5
- second_norm: float32 [128], replicated, may hold values from 0.25 to 1.75
- second_final: bfloat16 [128, 128], replicated, may hold values from -0.5 to 0.5
Outputs:
- pair_output: bfloat16 [768, 384, 128], P(('groups', 'dap'), ('chan', 'sub')), parts along dimension 0
There are 2 independent parts, one for each index of `groups`. A program takes and returns all parts, laid end to end along the dimension named above; an argument that names none is the same for every part. Nothing has to cross between parts.
All inputs are finite; a program needn't handle non-finite values.
Results may differ from a plain program's by a relative error of at most 0.013.
Values may be sent and summed in bfloat16 or wider, within the bound.
No kernel may reach another device: no remote copies, remote signals or barrier semaphores. Data moves between devices by JAX's collectives and lax.ppermute only.
A program may use at most 64 MiB of HBM per device.

v0:
```python
import jax
import jax.numpy as jnp
from jax import lax
from jax.sharding import PartitionSpec as P

epsilon = 1e-05


def layer_norm(values, norm_gain, reduce_axis):
    average = jnp.mean(values, axis=reduce_axis, keepdims=True)
    centred = values - average
    variance = jnp.mean(centred * centred, axis=reduce_axis, keepdims=True)
    return centred * lax.rsqrt(variance + epsilon) * norm_gain


def project_in(pair_state, norm_gain, project, gate_matrix):
    row_count, col_count, features = pair_state.shape
    flattened = pair_state.reshape(row_count * col_count, features).astype(jnp.float32)
    normed = layer_norm(flattened, norm_gain, 1).astype(jnp.bfloat16)
    projected = jnp.einsum("xc,cd->dx", normed, project, preferred_element_type=jnp.float32)
    left_part = jax.nn.sigmoid(projected[:features]) * projected[features : 2 * features]
    right_part = jax.nn.sigmoid(projected[2 * features : 3 * features]) * projected[3 * features :]
    left_part = left_part.astype(jnp.bfloat16).reshape(features, row_count, col_count)
    right_part = right_part.astype(jnp.bfloat16).reshape(features, row_count, col_count)
    gating = jax.nn.sigmoid(jnp.dot(normed, gate_matrix, preferred_element_type=jnp.float32))
    return (left_part, right_part, gating)


def finish(pair_state, mixture, gating, out_gain, final_matrix):
    features = mixture.shape[0]
    flattened = mixture.reshape(features, -1).astype(jnp.float32)
    normed = layer_norm(flattened, out_gain[:, None], 0).astype(jnp.bfloat16)
    update = jnp.einsum("cx,cd->xd", normed, final_matrix, preferred_element_type=jnp.float32)
    result = pair_state.reshape(-1, features).astype(jnp.float32) + gating * update
    return result.astype(jnp.bfloat16).reshape(pair_state.shape)


def shards(
    pair_input,
    first_gain,
    first_project,
    first_gate,
    first_norm,
    first_final,
    second_gain,
    second_project,
    second_gate,
    second_norm,
    second_final,
):
    left_part, right_part, gating = project_in(pair_input, first_gain, first_project, first_gate)
    left_part, right_part = (
        lax.all_to_all(left_part, ("chan", "sub"), split_axis=0, concat_axis=2, tiled=True),
        lax.all_to_all(right_part, ("chan", "sub"), split_axis=0, concat_axis=2, tiled=True),
    )
    mixture = jnp.einsum(
        "cik,cjk->cij",
        left_part,
        lax.all_gather(right_part, "dap", axis=1, tiled=True),
        preferred_element_type=jnp.float32,
    ).astype(jnp.bfloat16)
    mixture = lax.all_to_all(mixture, ("chan", "sub"), split_axis=2, concat_axis=0, tiled=True)
    middle = finish(pair_input, mixture, gating, first_norm, first_final)
    left_part, right_part, gating = project_in(middle, second_gain, second_project, second_gate)
    left_part, right_part = (
        lax.all_to_all(left_part, ("chan", "sub"), split_axis=0, concat_axis=2, tiled=True),
        lax.all_to_all(right_part, ("chan", "sub"), split_axis=0, concat_axis=2, tiled=True),
    )
    turned = lax.all_to_all(left_part, "dap", split_axis=2, concat_axis=1, tiled=True)
    mixture = jnp.einsum(
        "cki,ckj->cij",
        turned,
        lax.all_gather(right_part, "dap", axis=1, tiled=True),
        preferred_element_type=jnp.float32,
    )
    mixture = lax.all_to_all(
        mixture.astype(jnp.bfloat16), ("chan", "sub"), split_axis=2, concat_axis=0, tiled=True
    )
    return finish(middle, mixture, gating, second_norm, second_final)


def solution(mesh):
    placed = (
        P(("groups", "dap"), ("chan", "sub"), None),
        P(),
        P(),
        P(),
        P(),
        P(),
        P(),
        P(),
        P(),
        P(),
        P(),
    )
    return jax.shard_map(
        shards,
        mesh=mesh,
        in_specs=placed,
        out_specs=P(("groups", "dap"), ("chan", "sub"), None),
        check_vma=False,
    )
```

profile of v0, /device:TPU:0, one launch (start us, length us, event | category | flops | bytes accessed | tf_op | source)
XLA Modules:
  0.0 717.1 jit_solution(18188985698345366559)
XLA Ops:
  6.5 2.7 convert_reduce_fusion
  9.3 4.4 multiply_reduce_fusion.3
  13.7 0.1 div.49
  13.8 0.1 rsqrt.42
  13.9 4.9 fusion.29
  18.9 0.0 copy-start.6
  18.9 1.4 copy-done.6
  20.3 2.6 convolution_bitcast_fusion.1
  22.9 3.9 fusion.19
  26.8 4.8 copy.28
  31.6 41.2 %all_to_all.108 = bf16[128,96,96]{2,1,0:T(8,128)(2,1)S(1)} all-to-all(bf16[128,96,96]{2,1,0:T(8,128)(2,1)} %copy.28), channel_id=1, replica_groups=mesh['groups'=2,'dap'=4,'chan'=2,'sub'=2] {'chan','sub'}, dimensions={0} | all-to-all | bytes 4718592 | tf_op jit(solution)/shard_map/all_to_all | solution.py:54
  72.8 4.1 copy.29
  76.9 5.9 all_to_all.86
  82.9 0.0 all-gather.3.cloned.1.call-update
  82.9 4.8 copy.26
  87.7 53.0 %all_to_all.109 = bf16[128,96,96]{2,1,0:T(8,128)(2,1)S(1)} all-to-all(bf16[128,96,96]{2,1,0:T(8,128)(2,1)} %copy.26), channel_id=1, replica_groups=mesh['groups'=2,'dap'=4,'chan'=2,'sub'=2] {'chan','sub'}, dimensions={0} | all-to-all | bytes 4718592 | tf_op jit(solution)/shard_map/all_to_all | solution.py:53
  140.7 4.0 copy.27
  144.7 5.9 all_to_all.82
  150.7 100.2 %all-gather.3.cloned.1.call-done = bf16[32,384,384]{2,1,0:T(8,128)(2,1)} async-done(((bf16[32,96,384]{2,1,0:T(8,128)(2,1)}), bf16[32,384,384]{2,1,0:T(8,128)(2,1)}) %all-gather.3.cloned.1.call-update) | async-done | bytes 9437200 | tf_op jit(solution)/shard_map/all_gather | solution.py:59
  250.9 9.1 %convolution_convert_fusion.1 = bf16[32,96,384]{2,1,0:T(8,128)(2,1)} fusion(bf16[32,96,384]{2,1,0:T(8,128)(2,1)} %all_to_all.82, bf16[32,384,384]{2,1,0:T(8,128)(2,1)} %all-gather.3.cloned.1.call-done), kind=kOutput, calls=%fused_computation.61 | convolution fusion | flops 907149312 | bytes 14155776 | tf_op jit(solution)/shard_map/cik,cjk->cij/dot_general | solution.py:56
  260.0 5.0 copy.30
  265.0 4.7 all-to-all-start.2
  269.7 0.0 all-gather.5.cloned.1.call-start
  269.7 5.2 fusion.9
  274.9 31.7 %all-to-all-done.2 = bf16[32,96,384]{1,0,2:T(8,128)(2,1)} async-done(((bf16[32,96,384]{1,0,2:T(8,128)(2,1)}), bf16[32,96,384]{1,0,2:T(8,128)(2,1)}, u32[]{:S(2)}, u32[]{:S(2)}) %all-to-all-start.2) | async-done | bytes 2359328 | tf_op jit(solution)/shard_map/all_to_all | solution.py:62
  306.6 6.9 copy.31
  313.5 3.4 bitcast_reduce_fusion.1
  317.0 1.2 copy-done.2
  318.1 0.9 multiply_reduce_fusion.1
  319.0 0.1 div.55
  319.1 0.1 rsqrt.44
  319.2 0.0 copy-start.8
  319.2 7.2 %reshape.153 = f32[128,9216]{1,0:T(8,128)} reshape(f32[4,32,96,96]{3,2,1,0:T(8,128)} %bitcast.64) | data formatting | bytes 9437184 | tf_op jit(solution)/shard_map/convert_element_type | solution.py:31
  326.4 5.9 fusion.36
  332.4 2.7 multiply_reduce_fusion.2
  335.2 2.7 convolution_bitcast_fusion
  337.8 3.5 fusion.11
  341.4 4.7 copy.37
  346.1 40.8 %all_to_all.110 = bf16[128,96,96]{2,1,0:T(8,128)(2,1)S(1)} all-to-all(bf16[128,96,96]{2,1,0:T(8,128)(2,1)} %copy.37), channel_id=1, replica_groups=mesh['groups'=2,'dap'=4,'chan'=2,'sub'=2] {'chan','sub'}, dimensions={0} | all-to-all | bytes 4718592 | tf_op jit(solution)/shard_map/all_to_all | solution.py:67
  386.8 4.1 copy.38
  390.9 5.9 all_to_all.99
  396.9 0.0 all-gather.5.cloned.1.call-update
  396.9 3.2 copy.32
  400.1 42.3 %all_to_all.111 = bf16[128,96,96]{2,1,0:T(8,128)(2,1)} all-to-all(bf16[128,96,96]{2,1,0:T(8,128)(2,1)} %copy.32), channel_id=1, replica_groups=mesh['groups'=2,'dap'=4,'chan'=2,'sub'=2] {'chan','sub'}, dimensions={0} | all-to-all | bytes 4718592 | tf_op jit(solution)/shard_map/all_to_all | solution.py:66
  442.4 6.6 copy.41
  449.0 159.6 %all_to_all.112 = bf16[32,96,384]{1,0,2:T(8,128)(2,1)S(1)} all-to-all(bf16[32,96,384]{1,0,2:T(8,128)(2,1)} %bitcast.71), channel_id=1, replica_groups=mesh['groups'=2,'dap'=4,'chan'=2,'sub'=2] {'dap'}, dimensions={2} | all-to-all | bytes 4718592 | tf_op jit(solution)/shard_map/all_to_all | solution.py:69
  608.6 4.0 copy.46
  612.6 5.0 all_to_all.95
  617.6 10.6 %all-gather.5.cloned.1.call-done = bf16[32,384,384]{2,1,0:T(8,128)(2,1)} async-done(((bf16[32,96,384]{2,1,0:T(8,128)(2,1)}), bf16[32,384,384]{2,1,0:T(8,128)(2,1)}) %all-gather.5.cloned.1.call-update) | async-done | bytes 9437200 | tf_op jit(solution)/shard_map/all_gather | solution.py:73
  628.2 7.0 convolution_convert_fusion
  635.2 5.0 copy.39
  640.2 4.9 all-to-all-start.6
  645.1 6.7 fusion.10
  651.8 30.3 %all-to-all-done.6 = bf16[32,96,384]{1,0,2:T(8,128)(2,1)} async-done(((bf16[32,96,384]{1,0,2:T(8,128)(2,1)}), bf16[32,96,384]{1,0,2:T(8,128)(2,1)}, u32[]{:S(2)}, u32[]{:S(2)}) %all-to-all-start.6) | async-done | bytes 2359328 | tf_op jit(solution)/shard_map/all_to_all | solution.py:76
  682.1 6.9 copy.40
  689.0 3.4 bitcast_reduce_fusion
  692.4 1.2 copy-done.3
  693.6 0.9 multiply_reduce_fusion
  694.4 0.1 div.63
  694.6 0.1 rsqrt.47
  694.7 0.0 copy-start.13
  694.7 0.0 copy-start.1
  694.7 7.2 %reshape.154 = f32[128,9216]{1,0:T(8,128)} reshape(f32[4,32,96,96]{3,2,1,0:T(8,128)} %bitcast.65) | data formatting | bytes 9437184 | tf_op jit(solution)/shard_map/convert_element_type | solution.py:31
  701.9 8.0 %fusion.7 = bf16[9216,128]{1,0:T(8,128)(2,1)} fusion(f32[9216,128]{1,0:T(8,128)} %copy-done.4, f32[9216,128]{1,0:T(8,128)} %fusion.10, bf16[128,128]{1,0:T(8,128)(2,1)S(1)} %copy-done.9, f32[128,9216]{1,0:T(8,128)} %reshape.154, f32[128]{0:T(128)S(1)} %copy-done.13, f32[9216]{0:T(1024)S(1)} %rsqrt.47, f32[9216]{0:T(1024)S(1)} %div.63), kind=kOutput, calls=%fused_computation.13 | convolution fusion | flops 310247424 | bytes 16622080 | tf_op jit(solution)/shard_map/cx,cd->xd/dot_general | solution.py:33
  (34 shorter events, 0.1 us)
Async XLA Ops:
  6.5 13.7 %copy-start = (bf16[128,512]{1,0:T(8,128)(2,1)S(1)}, bf16[128,512]{1,0:T(8,128)(2,1)}, u32[]{:S(2)}) copy-start(bf16[128,512]{1,0:T(8,128)(2,1)} %param.13) | copy-start | bytes 393220
  6.5 7.3 %copy-start.5 = (bf16[96,96,128]{2,1,0:T(8,128)(2,1)S(1)}, bf16[96,96,128]{2,1,0:T(8,128)(2,1)}, u32[]{:S(2)}) copy-start(bf16[96,96,128]{2,1,0:T(8,128)(2,1)} %param.11) | copy-start | bytes 7077892
  6.5 7.3 %copy-start.12 = (f32[128]{0:T(128)S(1)}, f32[128]{0:T(128)}, u32[]{:S(2)}) copy-start(f32[128]{0:T(128)} %param.12) | copy-start | bytes 1540
  6.5 244.4 %all-gather.3.cloned.1.call-start = ((), (), s32[]{:S(2)}) async-start(), calls=%async_computation.7 | async-start | bytes 11796480 | tf_op jit(solution)/shard_map/all_gather | solution.py:59
  18.9 1.4 copy-start.6
  260.0 9.7 %copy-start.14 = (bf16[128,128]{1,0:T(8,128)(2,1)S(1)}, bf16[128,128]{1,0:T(8,128)(2,1)}, u32[]{:S(2)}) copy-start(bf16[128,128]{1,0:T(8,128)(2,1)} %param.14) | copy-start | bytes 98308
  265.0 41.6 %all-to-all-start.2 = ((bf16[32,96,384]{1,0,2:T(8,128)(2,1)}), bf16[32,96,384]{1,0,2:T(8,128)(2,1)}, u32[]{:S(2)}, u32[]{:S(2)}) async-start(bf16[32,96,384]{1,0,2:T(8,128)(2,1)} %copy.30), calls=%async_computation.2 | async-start | bytes 6291456 | tf_op jit(solution)/shard_map/all_to_all | solution.py:62
  269.7 358.5 %all-gather.5.cloned.1.call-start = ((), (), s32[]{:S(2)}) async-start(), calls=%async_computation.8 | async-start | bytes 11796480 | tf_op jit(solution)/shard_map/all_gather | solution.py:73
  313.5 4.6 copy-start.2
  319.2 7.2 %copy-start.8 = (bf16[128,128]{1,0:T(8,128)(2,1)S(1)}, bf16[128,128]{1,0:T(8,128)(2,1)}, u32[]{:S(2)}) copy-start(bf16[128,128]{1,0:T(8,128)(2,1)} %param.16) | copy-start | bytes 98308
  319.2 7.2 %copy-start.11 = (f32[128]{0:T(128)S(1)}, f32[128]{0:T(128)}, u32[]{:S(2)}) copy-start(f32[128]{0:T(128)} %param.15) | copy-start | bytes 1540
  332.3 5.5 copy-start.4
  332.4 2.8 copy-start.7
  332.4 2.8 copy-start.10
  635.2 9.9 %copy-start.15 = (bf16[128,128]{1,0:T(8,128)(2,1)S(1)}, bf16[128,128]{1,0:T(8,128)(2,1)}, u32[]{:S(2)}) copy-start(bf16[128,128]{1,0:T(8,128)(2,1)} %param.19) | copy-start | bytes 98308
  640.2 41.8 %all-to-all-start.6 = ((bf16[32,96,384]{1,0,2:T(8,128)(2,1)}), bf16[32,96,384]{1,0,2:T(8,128)(2,1)}, u32[]{:S(2)}, u32[]{:S(2)}) async-start(bf16[32,96,384]{1,0,2:T(8,128)(2,1)} %copy.39), calls=%async_computation.6 | async-start | bytes 6291456 | tf_op jit(solution)/shard_map/all_to_all | solution.py:76
  689.0 4.6 copy-start.3
  694.6 7.2 %copy-start.9 = (bf16[128,128]{1,0:T(8,128)(2,1)S(1)}, bf16[128,128]{1,0:T(8,128)(2,1)}, u32[]{:S(2)}) copy-start(bf16[128,128]{1,0:T(8,128)(2,1)} %param.21) | copy-start | bytes 98308
  694.7 7.2 %copy-start.13 = (f32[128]{0:T(128)S(1)}, f32[128]{0:T(128)}, u32[]{:S(2)}) copy-start(f32[128]{0:T(128)} %param.20) | copy-start | bytes 1540
  694.7 15.2 %copy-start.1 = (bf16[128,512]{1,0:T(8,128)(2,1)S(1)}, bf16[128,512]{1,0:T(8,128)(2,1)}, u32[]{:S(2)}) copy-start(bf16[128,512]{1,0:T(8,128)(2,1)} %param.13) | copy-start | bytes 393220
Sparse Core Ops, SparseCore 0:
  83.0 167.8 all-gather.2
  397.0 231.1 all-gather.4
where the time goes:
time: 727 us; the launch traced here: 717 us
  blocking collectives  337 us (46%)
  waiting for transfers between devices  173 us (24%)
  local copies, waits for them, and re-layouts  106 us (15%)
  matrix products  47 us (6%)
  other arithmetic  30.8 us (4%)
  between operations  14.1 us (2%)
  starting transfers between devices  9.58 us (1%)
    all_to_all x1, blocking collectives, shards(): lax.all_to_all(left_part, 'dap', split_axis=2, concat_axis=1, tiled=True)  160 us
    all_gather x2, waiting for transfers between devices, shards(): lax.all_gather(right_part, 'dap', axis=1, tiled=True)  111 us
    all_to_all x2, blocking collectives, shards(): lax.all_to_all(left_part, ('chan', 'sub'), split_axis=0, concat_axis=2, t...  95.4 us
    all_to_all x2, blocking collectives, shards(): lax.all_to_all(right_part, ('chan', 'sub'), split_axis=0, concat_axis=2,...  82 us
    all_to_all x1, waiting for transfers between devices, shards(): lax.all_to_all(mixture, ('chan', 'sub'), split_axis=2, concat_axis=0, til...  31.7 us
    all_to_all x1, waiting for transfers between devices, shards(): lax.all_to_all(mixture.astype(jnp.bfloat16), ('chan', 'sub'), split_axis=...  30.3 us
    convert_element_type x4, local copies, waits for them, and re-layouts, finish(): flattened = mixture.reshape(features, -1).astype(jnp.float32)  28.1 us
    all_to_all x4, local copies, waits for them, and re-layouts, shards(): lax.all_to_all(right_part, ('chan', 'sub'), split_axis=0, concat_axis=2,...  20 us
  transfers between devices with their start and end apart: 4, of which 4 were waited for; matrix products, arithmetic and copies ran while one was open for 5% of the time, Pallas kernels for 0%

commit v1 on v0

--- a/solution.py
+++ b/solution.py
@@ -4,6 +4,20 @@
 from jax.sharding import PartitionSpec as P
 
 epsilon = 1e-05
+
+
+def on_each_block(array, axis, dim, make, out_dim):
+    ways, here, hop = (lax.axis_size(axis), lax.axis_index(axis), array.shape[dim])
+    earlier, later = ([], [])
+    going_up = going_down = array
+    for far in range(ways // 2 + 1):
+        earlier.append(make(going_up, (here - far) % ways * hop))
+        if 0 < far < ways - ways // 2:
+            later.append(make(going_down, (here + far) % ways * hop))
+        going_up = lax.ppermute(going_up, axis, [(d, (d + 1) % ways) for d in range(ways)])
+        going_down = lax.ppermute(going_down, axis, [(d, (d - 1) % ways) for d in range(ways)])
+    line = jnp.concatenate([*earlier[::-1], *later], axis=out_dim)
+    return jnp.roll(line, (here - ways // 2) * earlier[0].shape[out_dim], axis=out_dim)
 
 
 def layer_norm(values, norm_gain, reduce_axis):
@@ -53,11 +67,14 @@
         lax.all_to_all(left_part, ("chan", "sub"), split_axis=0, concat_axis=2, tiled=True),
         lax.all_to_all(right_part, ("chan", "sub"), split_axis=0, concat_axis=2, tiled=True),
     )
-    mixture = jnp.einsum(
-        "cik,cjk->cij",
-        left_part,
-        lax.all_gather(right_part, "dap", axis=1, tiled=True),
-        preferred_element_type=jnp.float32,
+    mixture = on_each_block(
+        right_part,
+        "dap",
+        1,
+        lambda own_block, offset: jnp.einsum(
+            "cik,cjk->cij", left_part, own_block, preferred_element_type=jnp.float32
+        ),
+        2,
     ).astype(jnp.bfloat16)
     mixture = lax.all_to_all(mixture, ("chan", "sub"), split_axis=2, concat_axis=0, tiled=True)
     middle = finish(pair_input, mixture, gating, first_norm, first_final)

time: 727 us -> 703 us (0.967)
  blocking collectives: 337 us -> 281 us
  waiting for transfers between devices: 173 us -> 199 us
    ppermute x0 -> x3, waiting for transfers between devices: none -> 124 us  [the longest x2 89.6 us: on_each_block(): lax.ppermute(going_up, axis, [(d, (d + 1) % ways) for d in range(ways)])]
    all_gather x2 -> x1, waiting for transfers between devices: 111 us -> 13 us  [shards(): lax.all_gather(right_part, 'dap', axis=1, tiled=True)]
    all_to_all x2 -> x1, blocking collectives: 95.4 us -> 40.7 us  [shards(): lax.all_to_all(left_part, ('chan', 'sub'), split_axis=0, concat_axis=2, t...]
    concatenate x0 -> x1, local copies, waits for them, and re-layouts: none -> 9.59 us  [on_each_block(): jnp.roll(line, (here - ways // 2) * earlier[0].shape[out_dim], axis=out_dim)]
    all_to_all x4, local copies, waits for them, and re-layouts: 20 us -> 11.3 us  [shards(): lax.all_to_all(right_part, ('chan', 'sub'), split_axis=0, concat_axis=2,...]
  transfers between devices with their start and end apart: 4 -> 7, of which waited for: 4 -> 6; matrix products, arithmetic and copies ran while one was open for 5% -> 6% of each run, Pallas kernels for 0% -> 0%
where the time goes in v1:
time: 703 us; the launch traced here: 693 us
  blocking collectives  281 us (40%)
  waiting for transfers between devices  199 us (28%)
  local copies, waits for them, and re-layouts  101 us (14%)
  matrix products  51.3 us (7%)
  other arithmetic  31.2 us (4%)
  starting transfers between devices  15.9 us (2%)
  between operations  14.2 us (2%)
    all_to_all x1, blocking collectives, shards(): lax.all_to_all(left_part, 'dap', split_axis=2, concat_axis=1, tiled=True)  160 us
    ppermute x2, waiting for transfers between devices, on_each_block(): lax.ppermute(going_up, axis, [(d, (d + 1) % ways) for d in range(ways)])  89.6 us
    all_to_all x2, blocking collectives, shards(): lax.all_to_all(right_part, ('chan', 'sub'), split_axis=0, concat_axis=2,...  80.6 us
    all_to_all x1, blocking collectives, shards(): lax.all_to_all(left_part, ('chan', 'sub'), split_axis=0, concat_axis=2, t...  40.7 us
    ppermute x1, waiting for transfers between devices, on_each_block(): lax.ppermute(going_down, axis, [(d, (d - 1) % ways) for d in range(ways)])  34.7 us
    all_to_all x1, waiting for transfers between devices, shards(): lax.all_to_all(mixture, ('chan', 'sub'), split_axis=2, concat_axis=0, til...  31.4 us
    all_to_all x1, waiting for transfers between devices, shards(): lax.all_to_all(mixture.astype(jnp.bfloat16), ('chan', 'sub'), split_axis=...  30.2 us
    convert_element_type x4, local copies, waits for them, and re-layouts, finish(): flattened = mixture.reshape(features, -1).astype(jnp.float32)  24.2 us
  transfers between devices with their start and end apart: 7, of which 6 were waited for; matrix products, arithmetic and copies ran while one was open for 6% of the time, Pallas kernels for 0%

profile of v1, /device:TPU:0, one launch (start us, length us, event | category | flops | bytes accessed | tf_op | source)
XLA Modules:
  0.0 693.4 jit_solution(16365149354332728784)
XLA Ops:
  6.5 2.7 convert_reduce_fusion
  9.3 4.4 multiply_reduce_fusion.3
  13.8 0.1 rsqrt.42
  13.9 4.9 fusion.29
  18.9 1.4 copy-done.7
  20.3 2.6 convolution_bitcast_fusion.1
  22.9 3.9 fusion.19
  26.7 3.5 copy.28
  30.3 40.9 %all_to_all.108 = bf16[128,96,96]{2,1,0:T(8,128)(2,1)S(1)} all-to-all(bf16[128,96,96]{2,1,0:T(8,128)(2,1)S(1)} %copy.28), channel_id=1, replica_groups=mesh['groups'=2,'dap'=4,'chan'=2,'sub'=2] {'chan','sub'}, dimensions={0} | all-to-all | bytes 4718592 | tf_op jit(solution)/shard_map/all_to_all | solution.py:68
  71.2 2.4 copy.29
  73.7 3.2 all_to_all.86
  76.9 1.6 collective-permute-start
  78.5 4.8 copy.26
  83.2 3.7 all-to-all-start
  86.9 2.3 collective-permute-start.2
  89.2 43.9 %collective-permute-done = bf16[32,96,384]{2,1,0:T(8,128)(2,1)} collective-permute-done((bf16[32,96,384]{2,1,0:T(8,128)(2,1)}, bf16[32,96,384]{2,1,0:T(8,128)(2,1)}, u32[]{:S(2)}, u32[]{:S(2)}) %collective-permute-start) | collective-permute-done | bytes 2359328 | tf_op jit(solution)/shard_map/ppermute | solution.py:17
  133.2 0.5 collective-permute-start.1
  133.7 4.1 copy.27
  137.8 5.0 all_to_all.82
  142.8 2.7 fusion.39
  145.4 3.5 fusion.38
  149.0 34.7 %collective-permute-done.2 = bf16[32,96,384]{2,1,0:T(8,128)(2,1)} collective-permute-done((bf16[32,96,384]{2,1,0:T(8,128)(2,1)}, bf16[32,96,384]{2,1,0:T(8,128)(2,1)}, u32[]{:S(2)}, u32[]{:S(2)}) %collective-permute-start.2) | collective-permute-done | bytes 2359328 | tf_op jit(solution)/shard_map/ppermute | solution.py:18
  183.7 3.5 fusion.40
  187.2 45.7 %collective-permute-done.1 = bf16[32,96,384]{2,1,0:T(8,128)(2,1)} collective-permute-done((bf16[32,96,384]{2,1,0:T(8,128)(2,1)}, bf16[32,96,384]{2,1,0:T(8,128)(2,1)}, u32[]{:S(2)}, u32[]{:S(2)}) %collective-permute-start.1) | collective-permute-done | bytes 2359328 | tf_op jit(solution)/shard_map/ppermute | solution.py:17
  232.9 3.5 fusion.37
  236.4 9.6 %concatenate.6 = bf16[32,96,768]{2,1,0:T(8,128)(2,1)} concatenate(bf16[32,96,96]{2,1,0:T(8,128)(2,1)} %fusion.37, bf16[32,96,96]{2,1,0:T(8,128)(2,1)} %fusion.38, bf16[32,96,96]{2,1,0:T(8,128)(2,1)S(1)} %fusion.39, bf16[32,96,96]{2,1,0:T(8,128)(2,1)} %fusion.40, bf16[32,96,96]{2,1,0:T(8,128)(2,1)} %fusion.37, bf16[32,96,96]{2,1,0:T(8,128)(2,1)} %fusion.38, ...), dimensions={2} | concatenate | bytes 9437184 | tf_op jit(solution)/shard_map/jit(_roll_dynamic)/concatenate | solution.py:20
  246.0 3.2 dynamic-slice_convert_fusion
  249.2 3.5 copy.30
  252.6 3.7 all-to-all-start.2
  256.3 0.2 all-gather.2.cloned.1.call-start
  256.6 5.2 fusion.9
  261.8 31.4 %all-to-all-done.2 = bf16[32,96,384]{1,0,2:T(8,128)(2,1)S(1)} async-done(((bf16[32,96,384]{1,0,2:T(8,128)(2,1)}), bf16[32,96,384]{1,0,2:T(8,128)(2,1)S(1)}, u32[]{:S(2)}, u32[]{:S(2)}) %all-to-all-start.2) | async-done | bytes 2359328 | tf_op jit(solution)/shard_map/all_to_all | solution.py:79
  293.2 4.8 copy.31
  298.0 3.4 bitcast_reduce_fusion.1
  301.4 1.2 copy-done.2
  302.6 0.9 multiply_reduce_fusion.1
  303.6 0.1 rsqrt.44
  303.7 7.4 %reshape.153 = f32[128,9216]{1,0:T(8,128)} reshape(f32[4,32,96,96]{3,2,1,0:T(8,128)} %bitcast.70) | data formatting | bytes 9437184 | tf_op jit(solution)/shard_map/convert_element_type | solution.py:45
  311.1 5.9 fusion.36
  317.1 2.7 multiply_reduce_fusion.2
  319.9 2.7 convolution_bitcast_fusion
  322.6 3.9 fusion.11
  326.5 3.5 copy.37
  330.0 39.6 %all_to_all.109 = bf16[128,96,96]{2,1,0:T(8,128)(2,1)S(1)} all-to-all(bf16[128,96,96]{2,1,0:T(8,128)(2,1)S(1)} %copy.37), channel_id=1, replica_groups=mesh['groups'=2,'dap'=4,'chan'=2,'sub'=2] {'chan','sub'}, dimensions={0} | all-to-all | bytes 4718592 | tf_op jit(solution)/shard_map/all_to_all | solution.py:84
  369.6 2.4 copy.38
  372.1 3.2 all_to_all.99
  375.3 4.8 copy.32
  380.1 40.7 %all_to_all.110 = bf16[128,96,96]{2,1,0:T(8,128)(2,1)S(1)} all-to-all(bf16[128,96,96]{2,1,0:T(8,128)(2,1)} %copy.32), channel_id=1, replica_groups=mesh['groups'=2,'dap'=4,'chan'=2,'sub'=2] {'chan','sub'}, dimensions={0} | all-to-all | bytes 4718592 | tf_op jit(solution)/shard_map/all_to_all | solution.py:83
  420.8 5.2 copy.41
  426.0 159.7 %all_to_all.111 = bf16[32,96,384]{1,0,2:T(8,128)(2,1)S(1)} all-to-all(bf16[32,96,384]{1,0,2:T(8,128)(2,1)} %bitcast.77), channel_id=1, replica_groups=mesh['groups'=2,'dap'=4,'chan'=2,'sub'=2] {'dap'}, dimensions={2} | all-to-all | bytes 4718592 | tf_op jit(solution)/shard_map/all_to_all | solution.py:86
  585.7 4.1 copy.46
  589.8 5.0 all_to_all.95
  594.7 13.0 %all-gather.2.cloned.1.call-done = bf16[32,384,384]{2,1,0:T(8,128)(2,1)} async-done(((bf16[32,96,384]{2,1,0:T(8,128)(2,1)}), bf16[32,384,384]{2,1,0:T(8,128)(2,1)}) %all-gather.2.cloned.1.call-update) | async-done | bytes 9437200 | tf_op jit(solution)/shard_map/all_gather | solution.py:90
  607.7 7.0 %convolution_convert_fusion = bf16[32,96,384]{2,1,0:T(8,128)(2,1)} fusion(bf16[32,384,96]{1,2,0:T(8,128)(2,1)S(1)} %all_to_all.95, bf16[32,384,384]{2,1,0:T(8,128)(2,1)} %all-gather.2.cloned.1.call-done), kind=kOutput, calls=%fused_computation.61 | convolution fusion | flops 907149312 | bytes 14155776 | tf_op jit(solution)/shard_map/cki,ckj->cij/dot_general | solution.py:87
  614.7 4.9 copy.39
  619.6 4.0 all-to-all-start.6
  623.6 6.7 fusion.10
  630.3 30.2 %all-to-all-done.6 = bf16[32,96,384]{1,0,2:T(8,128)(2,1)S(1)} async-done(((bf16[32,96,384]{1,0,2:T(8,128)(2,1)}), bf16[32,96,384]{1,0,2:T(8,128)(2,1)S(1)}, u32[]{:S(2)}, u32[]{:S(2)}) %all-to-all-start.6) | async-done | bytes 2359328 | tf_op jit(solution)/shard_map/all_to_all | solution.py:93
  660.4 4.8 copy.40
  665.3 3.4 bitcast_reduce_fusion
  668.7 1.2 copy-done.3
  669.9 0.9 multiply_reduce_fusion
  671.0 7.2 %reshape.154 = f32[128,9216]{1,0:T(8,128)} reshape(f32[4,32,96,96]{3,2,1,0:T(8,128)} %bitcast.71) | data formatting | bytes 9437184 | tf_op jit(solution)/shard_map/convert_element_type | solution.py:45
  678.1 8.0 %fusion.7 = bf16[9216,128]{1,0:T(8,128)(2,1)} fusion(f32[9216,128]{1,0:T(8,128)} %copy-done.4, f32[9216,128]{1,0:T(8,128)} %fusion.10, bf16[128,128]{1,0:T(8,128)(2,1)S(1)} %copy-done.10, f32[128,9216]{1,0:T(8,128)} %reshape.154, f32[128]{0:T(128)S(1)} %copy-done.14, f32[9216]{0:T(1024)S(1)} %rsqrt.47, f32[9216]{0:T(1024)S(1)} %div.63), kind=kOutput, calls=%fused_computation.13 | convolution fusion | flops 310247424 | bytes 16622080 | tf_op jit(solution)/shard_map/cx,cd->xd/dot_general | solution.py:47
  (45 shorter events, 0.6 us)
Async XLA Ops:
  6.5 13.7 %copy-start = (bf16[128,512]{1,0:T(8,128)(2,1)S(1)}, bf16[128,512]{1,0:T(8,128)(2,1)}, u32[]{:S(2)}) copy-start(bf16[128,512]{1,0:T(8,128)(2,1)} %param.13) | copy-start | bytes 393220
  6.5 7.3 %copy-start.5 = (bf16[96,96,128]{2,1,0:T(8,128)(2,1)S(1)}, bf16[96,96,128]{2,1,0:T(8,128)(2,1)}, u32[]{:S(2)}) copy-start(bf16[96,96,128]{2,1,0:T(8,128)(2,1)} %param.11) | copy-start | bytes 7077892
  6.5 7.3 %copy-start.13 = (f32[128]{0:T(128)S(1)}, f32[128]{0:T(128)}, u32[]{:S(2)}) copy-start(f32[128]{0:T(128)} %param.12) | copy-start | bytes 1540
  18.8 1.4 copy-start.7
  76.9 56.3 %collective-permute-start = (bf16[32,96,384]{2,1,0:T(8,128)(2,1)}, bf16[32,96,384]{2,1,0:T(8,128)(2,1)}, u32[]{:S(2)}, u32[]{:S(2)}) collective-permute-start(bf16[32,96,384]{2,1,0:T(8,128)(2,1)} %all_to_all.86), channel_id=1, source_target_pairs={{0,4},{4,8},{8,12},{12,0},{1,5},{5,9},{9,13},{13,1},{2,6},{6,10},{... | collective-permute-start | bytes 7077896 | tf_op jit(solution)/shard_map/ppermute | solution.py:17
  83.2 50.5 %all-to-all-start = ((bf16[128,96,96]{2,1,0:T(8,128)(2,1)}), bf16[128,96,96]{2,1,0:T(8,128)(2,1)S(1)}, u32[]{:S(2)}, u32[]{:S(2)}) async-start(bf16[128,96,96]{2,1,0:T(8,128)(2,1)} %copy.26), calls=%async_computation | async-start | bytes 6291456 | tf_op jit(solution)/shard_map/all_to_all | solution.py:67
  86.9 96.7 %collective-permute-start.2 = (bf16[32,96,384]{2,1,0:T(8,128)(2,1)}, bf16[32,96,384]{2,1,0:T(8,128)(2,1)}, u32[]{:S(2)}, u32[]{:S(2)}) collective-permute-start(bf16[32,96,384]{2,1,0:T(8,128)(2,1)} %all_to_all.86), channel_id=1, source_target_pairs={{0,12},{4,0},{8,4},{12,8},{1,13},{5,1},{9,5},{13,9},{2,14},{6,2},{... | collective-permute-start | bytes 7077896 | tf_op jit(solution)/shard_map/ppermute | solution.py:18
  133.2 99.7 %collective-permute-start.1 = (bf16[32,96,384]{2,1,0:T(8,128)(2,1)}, bf16[32,96,384]{2,1,0:T(8,128)(2,1)}, u32[]{:S(2)}, u32[]{:S(2)}) collective-permute-start(bf16[32,96,384]{2,1,0:T(8,128)(2,1)} %collective-permute-done), channel_id=1, source_target_pairs={{0,4},{4,8},{8,12},{12,0},{1,5},{5,9},{9,13},{13,1},{2,6},{6,10},{... | collective-permute-start | bytes 7077896 | tf_op jit(solution)/shard_map/ppermute | solution.py:17
  249.2 7.4 %copy-start.15 = (bf16[128,128]{1,0:T(8,128)(2,1)S(1)}, bf16[128,128]{1,0:T(8,128)(2,1)}, u32[]{:S(2)}) copy-start(bf16[128,128]{1,0:T(8,128)(2,1)} %param.14) | copy-start | bytes 98308
  252.6 40.6 %all-to-all-start.2 = ((bf16[32,96,384]{1,0,2:T(8,128)(2,1)}), bf16[32,96,384]{1,0,2:T(8,128)(2,1)S(1)}, u32[]{:S(2)}, u32[]{:S(2)}) async-start(bf16[32,96,384]{1,0,2:T(8,128)(2,1)} %copy.30), calls=%async_computation.2 | async-start | bytes 6291456 | tf_op jit(solution)/shard_map/all_to_all | solution.py:79
  256.3 351.4 %all-gather.2.cloned.1.call-start = ((), (), s32[]{:S(2)}) async-start(), calls=%async_computation.7 | async-start | bytes 11796480 | tf_op jit(solution)/shard_map/all_gather | solution.py:90
  298.0 4.6 copy-start.2
  303.7 7.4 %copy-start.6 = (bf16[96,96,128]{2,1,0:T(8,128)(2,1)S(1)}, bf16[96,96,128]{2,1,0:T(8,128)(2,1)}, u32[]{:S(2)}) copy-start(bf16[96,96,128]{2,1,0:T(8,128)(2,1)} %param.11) | copy-start | bytes 7077892
  303.7 7.4 %copy-start.9 = (bf16[128,128]{1,0:T(8,128)(2,1)S(1)}, bf16[128,128]{1,0:T(8,128)(2,1)}, u32[]{:S(2)}) copy-start(bf16[128,128]{1,0:T(8,128)(2,1)} %param.16) | copy-start | bytes 98308
  303.7 7.4 %copy-start.12 = (f32[128]{0:T(128)S(1)}, f32[128]{0:T(128)}, u32[]{:S(2)}) copy-start(f32[128]{0:T(128)} %param.15) | copy-start | bytes 1540
  317.1 5.5 copy-start.4
  317.1 2.8 copy-start.8
  317.1 2.8 copy-start.11
  614.7 8.9 %copy-start.16 = (bf16[128,128]{1,0:T(8,128)(2,1)S(1)}, bf16[128,128]{1,0:T(8,128)(2,1)}, u32[]{:S(2)}) copy-start(bf16[128,128]{1,0:T(8,128)(2,1)} %param.19) | copy-start | bytes 98308
  619.6 40.8 %all-to-all-start.6 = ((bf16[32,96,384]{1,0,2:T(8,128)(2,1)}), bf16[32,96,384]{1,0,2:T(8,128)(2,1)S(1)}, u32[]{:S(2)}, u32[]{:S(2)}) async-start(bf16[32,96,384]{1,0,2:T(8,128)(2,1)} %copy.39), calls=%async_computation.6 | async-start | bytes 6291456 | tf_op jit(solution)/shard_map/all_to_all | solution.py:93
  665.3 4.6 copy-start.3
  670.9 7.2 %copy-start.10 = (bf16[128,128]{1,0:T(8,128)(2,1)S(1)}, bf16[128,128]{1,0:T(8,128)(2,1)}, u32[]{:S(2)}) copy-start(bf16[128,128]{1,0:T(8,128)(2,1)} %param.21) | copy-start | bytes 98308
  671.0 7.2 %copy-start.14 = (f32[128]{0:T(128)S(1)}, f32[128]{0:T(128)}, u32[]{:S(2)}) copy-start(f32[128]{0:T(128)} %param.20) | copy-start | bytes 1540
  671.0 15.1 %copy-start.1 = (bf16[128,512]{1,0:T(8,128)(2,1)S(1)}, bf16[128,512]{1,0:T(8,128)(2,1)}, u32[]{:S(2)}) copy-start(bf16[128,512]{1,0:T(8,128)(2,1)} %param.13) | copy-start | bytes 393220
Sparse Core Ops, SparseCore 0:
  375.4 232.2 all-gather.1
